TPU v7x, 32 devices: a whole 2x2x4 slice. The times are simulated.
32 devices in a mesh: sub: 4 (over y, x), row: 8 (over z, core).
Axes of the slice: x: 2, y: 2, z: 4, core: 2. Of those that a mesh axis runs over, the one named last changes fastest.
Arguments:
- inverse: float32 [4, 1024, 12288], P('sub', 'row')
- sources: float32 [4, 16, 12288], P('sub', None, 'row'), may hold values from -6 to 6
- line_history: float32 [4, 32, 1024], P('sub', None, 'row'), may hold values from -6 to 6
- line_dest: int32 [4, 1024], P('sub', 'row'), may hold values from 0 to 3, as said below
- line_port: int32 [4, 1024], P('sub', 'row'), may hold values from 0 to 1023
- line_delay: int32 [4, 1024], P('sub', 'row'), may hold values from 16 to 32
- prev_voltage: float32 [4, 1024], P('sub', 'row'), may hold values from -6 to 6
- flux_start: float32 [4, 1024], P('sub', 'row'), may hold values from -3 to 3
- arrester_gain: float32 [4, 1024], P('sub', 'row'), may hold values from 0.5 to 4
- core_gain: float32 [4, 1024], P('sub', 'row'), may hold values from 0.25 to 2
- arrester_slots: int32 [4, 128], P('sub', 'row'), may hold values from 0 to 127, as said below
- core_slots: int32 [4, 128], P('sub', 'row'), may hold values from 0 to 127, as said below
Outputs:
- voltages: float32 [4, 16, 1024], P('sub', None, 'row')
- final_flux: float32 [4, 1024], P('sub', 'row')
Inputs may be any that keep to these rules, and one draw needn't show every extreme that they name: `line_dest`: a record never names its own subnetwork; among the 128 records of one device no subnetwork is named more than 86 times, and in every such block some subnetwork is named exactly 86 times. `arrester_slots`: the 16 entries of one device are distinct slots of that device's 128 ports and share no slot with that device's core entries. `core_slots`: the 16 entries of one device are distinct slots of that device's 128 ports.
All inputs are finite; a program needn't handle non-finite values.
Results may differ from a plain program's by a relative error of at most 0.0003.
Values sent between devices are 32-bit elements; how exact they have to be, the bound alone decides.
A program may use at most 64 MiB of HBM per device.

v0:
```python
import jax
import jax.numpy as jnp
from jax import lax
from jax.sharding import PartitionSpec as P

STEPS = 16
HISTORY = 32
NEWTON = 2


half_step = 0.25
knee_volts = 1.5
cubic_term = 0.25


def element_terms(iterate, voltage, flux_now, arrester_mask, arrester_gain, core_mask, core_gain):
    linked = flux_now + half_step * (iterate + voltage)
    ratio = iterate / knee_volts
    current = arrester_mask * arrester_gain * iterate * (
        1.0 + ratio * ratio
    ) + core_mask * core_gain * (linked + cubic_term * linked * linked * linked)
    slope_now = arrester_mask * arrester_gain * (
        1.0 + 3.0 * ratio * ratio
    ) + core_mask * core_gain * half_step * (1.0 + 3.0 * cubic_term * linked * linked)
    return (current, slope_now)


def on_device(
    inverse,
    sources,
    line_history,
    line_dest,
    line_port,
    line_delay,
    prev_voltage,
    flux_start,
    arrester_gain,
    core_gain,
    arrester_slots,
    core_slots,
):
    matrix = inverse[0]
    port_rows = matrix.shape[0]
    row_count = lax.axis_size("row")
    slice_len = sources.shape[2]
    subnets = lax.axis_size("sub")
    lines_here = line_dest.shape[1]
    capacity = 2 * ((lines_here + subnets - 2) // (subnets - 1))
    target = line_dest[0]
    onehot_dest = (target[:, None] == jnp.arange(subnets, dtype=jnp.int32)[None, :]).astype(
        jnp.int32
    )
    running_rank = jnp.cumsum(onehot_dest, axis=0)
    within = jnp.sum(onehot_dest * running_rank, axis=1) - 1
    position = target * capacity + within
    placing = position[:, None] == jnp.arange(subnets * capacity, dtype=jnp.int32)[None, :]
    place_float = placing.astype(jnp.float32).reshape(lines_here, subnets, capacity)
    place_int = placing.astype(jnp.int32).reshape(lines_here, subnets, capacity)
    outgoing = jnp.einsum(
        "hl,lsc->shc", line_history[0], place_float, precision=lax.Precision.HIGHEST
    )
    port_slot = jnp.sum(place_int * (line_port[0] + 1)[:, None, None], axis=0) - 1
    delay_slot = jnp.sum(place_int * line_delay[0][:, None, None], axis=0)
    tag_block = jnp.stack([port_slot, delay_slot], axis=1)
    arrived, arrived_tags = (
        lax.all_to_all(outgoing, "sub", split_axis=0, concat_axis=0, tiled=True),
        lax.all_to_all(tag_block, "sub", split_axis=0, concat_axis=0, tiled=True),
    )
    records = subnets * capacity
    arrived_hist = jnp.transpose(arrived, (1, 0, 2)).reshape(HISTORY, records)
    arrived_port = arrived_tags[:, 0, :].reshape(records)
    arrived_delay = arrived_tags[:, 1, :].reshape(records)
    lag_index = HISTORY + jnp.arange(STEPS, dtype=jnp.int32)[:, None] - arrived_delay[None, :]
    lag_hit = jnp.arange(HISTORY, dtype=jnp.int32)[:, None, None] == lag_index[None, :, :]
    picked = jnp.sum(jnp.where(lag_hit, arrived_hist[:, None, :], 0.0), axis=0)
    landing = (
        arrived_port[:, None] == jnp.arange(row_count * port_rows, dtype=jnp.int32)[None, :]
    ).astype(jnp.float32)
    partial_value = -jnp.dot(picked, landing, precision=lax.Precision.HIGHEST)
    history = lax.psum_scatter(partial_value, "row", scatter_dimension=1, tiled=True)
    row_index = lax.axis_index("row")
    own_block = lax.dynamic_slice_in_dim(matrix, row_index * slice_len, port_rows, 1)
    self_imp = jnp.diagonal(own_block)
    arrest_here = arrester_gain[0]
    core_here = core_gain[0]
    source_rows = sources[0]
    window = jnp.concatenate(
        [source_rows[:, :port_rows] + history, source_rows[:, port_rows:]], axis=1
    )
    first_terms = lax.dot_general(
        lax.all_gather(window, "row", axis=1, tiled=True),
        matrix,
        (((1,), (1,)), ((), ())),
        precision=lax.Precision.HIGHEST,
    )
    coupling = matrix.reshape(port_rows, row_count, slice_len)[:, :, :port_rows].reshape(
        port_rows, row_count * port_rows
    )
    elem_slots = jnp.concatenate([arrester_slots[0], core_slots[0]])
    elem_count = elem_slots.shape[0]
    all_slots = lax.all_gather(elem_slots, "row", axis=0, tiled=True)
    global_ports = (
        jnp.arange(all_slots.shape[0], dtype=jnp.int32) // elem_count * port_rows + all_slots
    )
    cross_cols = jnp.take(coupling, global_ports, axis=1)
    own_rows = jnp.take(cross_cols, elem_slots, axis=0)
    arrest_flag = (jnp.arange(elem_count, dtype=jnp.int32) < arrester_slots.shape[1]).astype(
        jnp.float32
    )
    local_params = jnp.stack(
        [
            arrest_here[elem_slots],
            core_here[elem_slots],
            prev_voltage[0][elem_slots],
            flux_start[0][elem_slots],
            self_imp[elem_slots],
            arrest_flag,
        ],
        axis=1,
    )
    local_first = jnp.transpose(jnp.take(first_terms, elem_slots, axis=1))
    elem_matrix, elem_first, elem_params = (
        lax.all_gather(own_rows, "row", axis=0, tiled=True),
        lax.all_gather(local_first, "row", axis=0, tiled=True),
        lax.all_gather(local_params, "row", axis=0, tiled=True),
    )
    arrest_elem = elem_params[:, 0]
    core_elem = elem_params[:, 1]
    elem_self = elem_params[:, 4]
    elem_arrest = elem_params[:, 5]
    elem_core = 1.0 - elem_arrest

    def elem_advance(carried, first_now):
        voltage, flux_now = carried
        iterate = voltage
        current = jnp.zeros_like(voltage)
        for newton_pass in range(NEWTON):
            current, slope_now = element_terms(
                iterate, voltage, flux_now, elem_arrest, arrest_elem, elem_core, core_elem
            )
            network = first_now - jnp.dot(elem_matrix, current, precision=lax.Precision.HIGHEST)
            iterate = iterate - (iterate - network) / (1.0 + elem_self * slope_now)
        return ((iterate, flux_now + half_step * (iterate + voltage)), (iterate, current))

    (elem_last, elem_flux), (elem_volts, last_current) = lax.scan(
        elem_advance, (elem_params[:, 2], elem_params[:, 3]), jnp.transpose(elem_first)
    )
    own_volts = first_terms - lax.dot_general(
        last_current, cross_cols, (((1,), (1,)), ((), ())), precision=lax.Precision.HIGHEST
    )
    own_elem = lax.dynamic_slice_in_dim(elem_volts, row_index * elem_count, elem_count, 1)
    elem_place = (elem_slots[:, None] == jnp.arange(port_rows, dtype=jnp.int32)[None, :]).astype(
        jnp.float32
    )
    elem_here = jnp.sum(elem_place, axis=0)
    stacked = own_volts * (1.0 - elem_here) + jnp.dot(
        own_elem, elem_place, precision=lax.Precision.HIGHEST
    )
    previous = jnp.concatenate([prev_voltage[0][None, :], stacked[:-1]], axis=0)
    final_flux = flux_start[0] + half_step * jnp.sum(stacked + previous, axis=0)
    return (stacked[None], final_flux[None])


def solution(mesh):
    in_specs = (
        P("sub", "row", None),
        P("sub", None, "row"),
        P("sub", None, "row"),
        P("sub", "row"),
        P("sub", "row"),
        P("sub", "row"),
        P("sub", "row"),
        P("sub", "row"),
        P("sub", "row"),
        P("sub", "row"),
        P("sub", "row"),
        P("sub", "row"),
    )
    out_specs = (P("sub", None, "row"), P("sub", "row"))
    return jax.shard_map(
        on_device, mesh=mesh, in_specs=in_specs, out_specs=out_specs, check_vma=False
    )
```

profile of v0, /device:TPU:0, one launch (start us, length us, event | category | flops | bytes accessed | tf_op | source)
XLA Modules:
  0.0 157.2 jit_solution(13829604152136079206)
XLA Ops:
  7.2 0.7 fusion.25
  8.1 0.8 select_reduce_fusion.1
  8.9 0.7 add_add_fusion
  9.6 0.7 add_bitcast_fusion
  10.3 1.0 fusion.19
  11.2 0.6 pad_add_fusion
  11.8 5.2 %all-to-all-start = ((s32[4,2,86]{2,1,0:T(2,128)}), s32[4,2,86]{2,1,0:T(2,128)S(1)}, u32[]{:S(2)}, u32[]{:S(2)}) async-start(s32[4,2,86]{2,1,0:T(2,128)} %pad_add_fusion), calls=%async_computation | async-start | bytes 8192 | tf_op jit(solution)/shard_map/all_to_all | solution.py:67
  17.1 1.2 dynamic-slice.1
  19.0 0.8 fusion.36
  20.0 6.6 %copy.44 = f32[1,128,12288]{1,2,0:T(8,128)} copy(f32[1,128,12288]{2,1,0:T(8,128)} %param.14) | data formatting | bytes 12582912 | tf_op jit(solution)/shard_map/reshape;squeeze | solution.py:96
  26.6 0.9 dynamic-slice_bitcast_fusion
  27.6 1.2 gather_fusion.4
  28.8 0.7 gather_fusion.5
  29.5 0.7 gather_fusion
  30.2 0.7 gather_fusion.1
  30.9 0.7 gather_fusion.2
  31.6 0.7 gather_fusion.3
  32.4 14.3 %all-gather = f32[8,32,6]{1,2,0:T(8,128)S(1)} all-gather(f32[1,32,6]{1,2,0:T(8,128)S(1)} %bitcast.120), channel_id=1, replica_groups=mesh['sub'=4,'row'=8] {'row'}, dimensions={0}, use_global_device_ids=true | all-gather | bytes 6912 | tf_op jit(solution)/shard_map/all_gather | solution.py:125
  46.8 1.0 convolution_bitcast_fusion
  47.8 8.9 %all-reduce = s32[256]{0:T(256)S(1)} all-reduce(s32[256]{0:T(256)S(1)} %get-tuple-element.216), channel_id=1, replica_groups=mesh['sub'=4,'row'=8] {'row'}, use_global_device_ids=true, to_apply=%add | all-reduce | flops 256 | bytes 2048
  56.7 1.1 slice.75
  57.8 0.7 gather_fusion.7
  58.8 0.6 gather_fusion.8
  59.4 4.2 %all-to-all-start.1 = ((f32[4,32,86]{2,1,0:T(8,128)}), f32[4,32,86]{2,1,0:T(8,128)S(1)}, u32[]{:S(2)}, u32[]{:S(2)}) async-start(f32[4,32,86]{2,1,0:T(8,128)} %convolution_bitcast_fusion), calls=%async_computation.1 | async-start | bytes 131072 | tf_op jit(solution)/shard_map/all_to_all | solution.py:66
  63.9 4.6 %all-to-all-done.1 = f32[4,32,86]{2,1,0:T(8,128)S(1)} async-done(((f32[4,32,86]{2,1,0:T(8,128)}), f32[4,32,86]{2,1,0:T(8,128)S(1)}, u32[]{:S(2)}, u32[]{:S(2)}) %all-to-all-start.1) | async-done | bytes 44064 | tf_op jit(solution)/shard_map/all_to_all | solution.py:66
  68.7 1.2 fusion.15
  70.1 14.2 %all_gather.19 = f32[256,256]{1,0:T(8,128)S(1)} all-gather(f32[32,256]{1,0:T(8,128)S(1)} %broadcast_select_fusion), channel_id=1, replica_groups=mesh['sub'=4,'row'=8] {'row'}, dimensions={0}, use_global_device_ids=true | all-gather | bytes 294912 | tf_op jit(solution)/shard_map/all_gather | solution.py:123
  84.3 13.3 %reduce-scatter.2.cloned.1.call-done = f32[16,128]{1,0:T(8,128)} async-done(((f32[16,1024]{1,0:T(8,128)}), f32[16,128]{1,0:T(8,128)}) %reduce-scatter.2.cloned.1.call-update) | async-done | bytes 8208 | tf_op jit(solution)/shard_map/reduce_scatter | solution.py:80
  97.6 0.7 slice_add_fusion
  98.3 15.7 %all_gather.15 = f32[16,12288]{1,0:T(8,128)S(1)} all-gather(f32[16,1536]{1,0:T(8,128)S(1)} %pad_maximum_fusion), channel_id=1, replica_groups=mesh['sub'=4,'row'=8] {'row'}, dimensions={1}, use_global_device_ids=true | all-gather | bytes 884736 | tf_op jit(solution)/shard_map/all_gather | solution.py:91
  114.0 7.0 %fusion.12 = f32[16,128]{1,0:T(8,128)S(1)} fusion(f32[16,12288]{1,0:T(8,128)S(1)} %all_gather.15, f32[1,128,12288]{2,1,0:T(8,128)} %param.14), kind=kOutput, calls=%fused_computation.31 | convolution fusion | flops 301989888 | bytes 7086080 | tf_op jit(solution)/shard_map/dot_general | solution.py:90
  121.1 0.6 gather_fusion.6
  121.8 14.0 %all-gather.1 = f32[8,32,16]{1,2,0:T(8,128)S(1)} all-gather(f32[1,32,16]{1,2,0:T(8,128)S(1)} %copy.40), channel_id=1, replica_groups=mesh['sub'=4,'row'=8] {'row'}, dimensions={0}, use_global_device_ids=true | all-gather | bytes 18432 | tf_op jit(solution)/shard_map/all_gather | solution.py:124
  135.9 13.4 %while.19 = (s32[]{:T(128)}, f32[256]{0:T(256)S(1)}, f32[256]{0:T(256)S(1)}, f32[16,256]{1,0:T(8,128)S(1)}, f32[16,256]{1,0:T(8,128)S(1)}, /*index=5*/f32[16,256...) while((s32[]{:T(128)}, f32[256]{0:T(256)S(1)}, ...), condition=%wide.region_7.8_spmd, body=%wide.region_6.7_spmd.sunk | while | flops 1591042 | bytes 559233 | solution.py:145
  136.3 0.3 fusion.62
  137.1 0.3 fusion.62
  138.0 0.3 fusion.62
  138.8 0.3 fusion.62
  139.6 0.3 fusion.62
  140.5 0.3 fusion.62
  141.3 0.3 fusion.62
  142.2 0.3 fusion.62
  143.0 0.3 fusion.62
  143.8 0.3 fusion.62
  144.7 0.3 fusion.62
  145.5 0.3 fusion.62
  146.3 0.3 fusion.62
  149.8 0.5 bitcast_add_fusion
  (176 shorter events, 11.6 us)
Async XLA Ops:
  7.2 39.6 %copy-start = (f32[1,32,128]{2,1,0:T(8,128)S(1)}, f32[1,32,128]{2,1,0:T(8,128)}, u32[]{:S(2)}) copy-start(f32[1,32,128]{2,1,0:T(8,128)} %param.16) | copy-start | bytes 49156
  11.8 47.6 %all-to-all-start = ((s32[4,2,86]{2,1,0:T(2,128)}), s32[4,2,86]{2,1,0:T(2,128)S(1)}, u32[]{:S(2)}, u32[]{:S(2)}) async-start(s32[4,2,86]{2,1,0:T(2,128)} %pad_add_fusion), calls=%async_computation | async-start | bytes 8192 | tf_op jit(solution)/shard_map/all_to_all | solution.py:67
  19.9 7.6 %copy-start.7 = (s32[1,16]{1,0:T(1,128)S(1)}, s32[1,16]{1,0:T(1,128)}, u32[]{:S(2)}) copy-start(s32[1,16]{1,0:T(1,128)} %param.25) | copy-start | bytes 196
  19.9 7.6 %copy-start.8 = (s32[1,16]{1,0:T(1,128)S(1)}, s32[1,16]{1,0:T(1,128)}, u32[]{:S(2)}) copy-start(s32[1,16]{1,0:T(1,128)} %param.24) | copy-start | bytes 196
  19.9 9.6 %copy-start.2 = (f32[1,128]{1,0:T(1,128)S(1)}, f32[1,128]{1,0:T(1,128)}, u32[]{:S(2)}) copy-start(f32[1,128]{1,0:T(1,128)} %param.22) | copy-start | bytes 1540
  19.9 10.3 %copy-start.3 = (f32[1,128]{1,0:T(1,128)S(1)}, f32[1,128]{1,0:T(1,128)}, u32[]{:S(2)}) copy-start(f32[1,128]{1,0:T(1,128)} %param.23) | copy-start | bytes 1540
  19.9 11.0 %copy-start.1 = (f32[1,128]{1,0:T(1,128)S(1)}, f32[1,128]{1,0:T(1,128)}, u32[]{:S(2)}) copy-start(f32[1,128]{1,0:T(1,128)} %param.20) | copy-start | bytes 1540
  20.0 11.7 %copy-start.4 = (f32[1,128]{1,0:T(1,128)S(1)}, f32[1,128]{1,0:T(1,128)}, u32[]{:S(2)}) copy-start(f32[1,128]{1,0:T(1,128)} %param.21) | copy-start | bytes 1540
  26.6 43.5 %copy-start.5 = (f32[1,16,1536]{2,1,0:T(8,128)S(1)}, f32[1,16,1536]{2,1,0:T(8,128)}, u32[]{:S(2)}) copy-start(f32[1,16,1536]{2,1,0:T(8,128)} %param.15) | copy-start | bytes 294916
  59.4 9.0 %all-to-all-start.1 = ((f32[4,32,86]{2,1,0:T(8,128)}), f32[4,32,86]{2,1,0:T(8,128)S(1)}, u32[]{:S(2)}, u32[]{:S(2)}) async-start(f32[4,32,86]{2,1,0:T(8,128)} %convolution_bitcast_fusion), calls=%async_computation.1 | async-start | bytes 131072 | tf_op jit(solution)/shard_map/all_to_all | solution.py:66
  63.6 33.9 %reduce-scatter.2.cloned.1.call-start = ((), (), s32[]{:S(2)}) async-start(), calls=%async_computation.3 | async-start | bytes 73728 | tf_op jit(solution)/shard_map/reduce_scatter | solution.py:80
  149.8 0.6 copy-start.6
Sparse Core Ops, SparseCore 0:
  70.1 27.3 reduce-scatter.1
where the time goes:
time: 158 us; the launch traced here: 157 us
  blocking collectives  67.2 us (43%)
  local copies, waits for them, and re-layouts  19.8 us (13%)
  matrix products  18.1 us (11%)
  waiting for transfers between devices  17.9 us (11%)
  between operations  14.9 us (9%)
  other arithmetic  9.39 us (6%)
  starting transfers between devices  9.39 us (6%)
    all_gather x1, blocking collectives, on_device(): lax.all_gather(window, 'row', axis=1, tiled=True)  15.7 us
    all_gather x1, blocking collectives, on_device(): lax.all_gather(local_params, 'row', axis=0, tiled=True)  14.3 us
    all_gather x1, blocking collectives, on_device(): lax.all_gather(own_rows, 'row', axis=0, tiled=True)  14.2 us
    all_gather x1, blocking collectives, on_device(): lax.all_gather(local_first, 'row', axis=0, tiled=True)  14 us
    reduce_scatter x1, waiting for transfers between devices, on_device(): lax.psum_scatter(partial_value, 'row', scatter_dimension=1, tiled=True)  13.3 us
    unnamed x1, blocking collectives  8.92 us
    dot_general x32, matrix products, elem_advance(): jnp.dot(elem_matrix, current, precision=lax.Precision.HIGHEST)  8.45 us
    dot_general x1, matrix products, on_device(): lax.dot_general(lax.all_gather(window, 'row', axis=1, tiled=True), matrix...  6.97 us
  transfers between devices with their start and end apart: 3, of which 2 were waited for; matrix products, arithmetic and copies ran while one was open for 12% of the time, Pallas kernels for 0%

commit v1 on v0

v1 whole, which is shorter than its diff:
```python
import functools

import jax
import jax.numpy as jnp
from jax import lax
from jax.experimental import pallas as pl
from jax.experimental.pallas import tpu as pltpu
from jax.sharding import PartitionSpec as P

STEPS = 16
HISTORY = 32
NEWTON = 2
CHUNKS = 2
LANES = 128

half_step = 0.25
knee_volts = 1.5
cubic_term = 0.25

F32 = jnp.float32
BF16 = jnp.bfloat16
MESH = pl.DeviceIdType.MESH
NN = (((1,), (0,)), ((), ()))
NT = (((1,), (1,)), ((), ()))
HIGHEST = lax.Precision.HIGHEST


def iota(shape, axis):
    return lax.broadcasted_iota(jnp.int32, shape, axis)


def hi_lo(x):
    high = x.astype(BF16)
    return high, (x - high.astype(F32)).astype(BF16)


def stack_hi_lo(x):
    return jnp.concatenate(hi_lo(x), axis=0)


def dot(a, b, dims=NN):
    return lax.dot_general(a, b, dims, preferred_element_type=F32)


def four_terms(r):
    n, m = r.shape[0] // 2, r.shape[1] // 2
    return (r[:n, :m] + r[n:, :m]) + (r[:n, m:] + r[n:, m:])


def kernel(
    subs, rows, ports, slice_len, arrests, cores,
    inv, src, hist, dest, port, delay, prev, flux, again, cgain, aslots, cslots,
    out, fout,
    m32, m2, gath, rec, elem, par, fst, recout, x2, wc, fall, vo, cu, acc, hacc,
    inv_sem, src_sem, line_send, line_recv, rec_send, rec_recv, par_send, par_recv,
    elem_send, elem_recv, fst_send, fst_recv,
):
    s = lax.axis_index("sub")
    me = lax.axis_index("row")
    z, c = me // 2, me % 2
    zn = rows // 2
    partner = z * 2 + (1 - c)
    elems = arrests + cores
    group = LANES // elems
    total = rows * elems
    halves = total // LANES
    width = slice_len // CHUNKS

    barrier = pltpu.get_barrier_semaphore()
    for j in range(1, rows):
        pl.semaphore_signal(barrier, inc=1, device_id=(s, lax.rem(me + j, rows)), device_id_type=MESH)
    for j in range(1, subs):
        pl.semaphore_signal(barrier, inc=1, device_id=(lax.rem(s + j, subs), me), device_id_type=MESH)

    for k in range(CHUNKS):
        pltpu.make_async_copy(
            src.at[0, :, pl.ds(k * width, width)], gath.at[k, me], src_sem.at[k]
        ).start()

    def inv_copy(r):
        cols = pl.ds(pl.multiple_of(r * slice_len, LANES), slice_len)
        return pltpu.make_async_copy(inv.at[0, :, cols], m32.at[:, cols], inv_sem.at[r])

    for r in range(rows):
        inv_copy(r).start()

    shifted = hist[0]
    shift = HISTORY - delay[...]
    bit = 1
    while bit <= HISTORY - STEPS:
        moved = pltpu.roll(shifted, HISTORY - bit, 0)
        shifted = jnp.where((shift // bit) % 2 == 1, moved, shifted)
        bit *= 2
    recout[:STEPS, :] = shifted[:STEPS, :]
    recout[STEPS:, :] = jnp.broadcast_to((dest[...] * (rows * ports) + port[...]).astype(F32), (8, LANES))

    lane16a, row16a = iota((arrests, LANES), 1), iota((arrests, LANES), 0)
    lane16c, row16c = iota((cores, LANES), 1), iota((cores, LANES), 0)
    put_a = jnp.where(lane16a % elems == row16a, 1.0, 0.0).astype(BF16)
    put_c = jnp.where(lane16c % elems == row16c + arrests, 1.0, 0.0).astype(BF16)
    slot_a = jnp.broadcast_to(aslots[...].astype(F32), (8, arrests)).astype(BF16)
    slot_c = jnp.broadcast_to(cslots[...].astype(F32), (8, cores)).astype(BF16)
    slot_row = (dot(slot_a, put_a) + dot(slot_c, put_c))[0:1, :]
    hit = iota((ports, LANES), 0).astype(F32) == slot_row
    slot_tiled = jnp.where(hit, 1.0, 0.0)
    slot_own = jnp.where(iota((ports, LANES), 1) // elems == me % group, slot_tiled, 0.0)
    r8 = iota((8, ports), 0)
    params = jnp.where(
        r8 == 0,
        iota((8, ports), 1).astype(F32),
        jnp.where(
            r8 == 1,
            again[...],
            jnp.where(r8 == 2, cgain[...], jnp.where(r8 == 3, prev[...], flux[...])),
        ),
    )
    par[me] = lax.dot_general(params, slot_own, NN, precision=HIGHEST, preferred_element_type=F32)

    pl.semaphore_wait(barrier, rows + subs - 2)

    def line_copy(kind, b, way, target):
        ref = rec.at[b] if kind == CHUNKS else gath.at[kind, b]
        return pltpu.make_async_remote_copy(
            src_ref=ref, dst_ref=ref, send_sem=line_send.at[kind, b, way],
            recv_sem=line_recv.at[kind, b], device_id=(s, target), device_id_type=MESH,
        )

    def own_sends(kind):
        @pl.when(z + 1 < zn)
        def _():
            line_copy(kind, me, 0, me + 2).start()

        @pl.when(z > 0)
        def _():
            line_copy(kind, me, 1, me - 2).start()

        line_copy(kind, me, 2, partner).start()

    for j in range(1, subs):
        to = lax.rem(s + j, subs)
        pltpu.make_async_remote_copy(
            src_ref=recout, dst_ref=rec.at[me, subs - 1 - j], send_sem=rec_send.at[j - 1],
            recv_sem=rec_recv.at[subs - 1 - j], device_id=(to, me), device_id_type=MESH,
        ).start()
    for j in range(1, rows):
        pltpu.make_async_remote_copy(
            src_ref=par.at[me], dst_ref=par.at[me], send_sem=par_send.at[j - 1],
            recv_sem=par_recv.at[me], device_id=(s, lax.rem(me + j, rows)), device_id_type=MESH,
        ).start()
    for k in range(CHUNKS):
        pltpu.make_async_copy(
            src.at[0, :, pl.ds(k * width, width)], gath.at[k, me], src_sem.at[k]
        ).wait()
        own_sends(k)

    def split_matrix(r, carry):
        inv_copy(r).wait()
        cols = pl.ds(pl.multiple_of(r * slice_len, LANES), slice_len)
        high, low = hi_lo(m32[:, cols])
        m2[:ports, cols] = high
        m2[ports:, cols] = low
        return carry

    early = min(2, rows)
    lax.fori_loop(0, early, split_matrix, 0)

    for j in range(subs - 1):
        pltpu.make_async_remote_copy(
            src_ref=recout, dst_ref=rec.at[me, j], send_sem=rec_send.at[j],
            recv_sem=rec_recv.at[j], device_id=(s, me), device_id_type=MESH,
        ).wait_recv()
    own_sends(CHUNKS)
    lax.fori_loop(early, rows, split_matrix, 0)

    for j in range(1, rows):
        b = lax.rem(me + j, rows)
        pltpu.make_async_remote_copy(
            src_ref=par.at[b], dst_ref=par.at[b], send_sem=par_send.at[j - 1],
            recv_sem=par_recv.at[b], device_id=(s, b), device_id_type=MESH,
        ).wait_recv()
    all_par = jnp.concatenate(
        [sum(par[h * group + i] for i in range(group)) for h in range(halves)], axis=1
    )
    slots_all = all_par[0:1, :]
    at_slot = iota((ports, total), 0).astype(F32) == slots_all
    owner_of = iota((ports, total), 1) // elems
    pick = None
    for r in range(rows):
        choose = jnp.where(jnp.logical_and(at_slot, owner_of == r), 1.0, 0.0).astype(BF16)
        term = dot(m2[:, r * slice_len : r * slice_len + ports], choose)
        pick = term if pick is None else pick + term
    x2[...] = pick.astype(BF16)
    slot_cols = jnp.transpose(slot_tiled)[:elems].astype(BF16)
    elem[me] = dot(slot_cols, x2[:ports, :]) + dot(slot_cols, x2[ports:, :])

    def elem_copy(b, sem_at, target):
        return pltpu.make_async_remote_copy(
            src_ref=elem.at[b], dst_ref=elem.at[b], send_sem=elem_send.at[sem_at],
            recv_sem=elem_recv.at[b], device_id=(s, target), device_id_type=MESH,
        )

    for j in range(1, zn):
        elem_copy(me, zn + j - 1, lax.rem(z + j, zn) * 2 + c).start()
    elem_copy(me, z, partner).start()

    acc[...] = jnp.zeros_like(acc)
    hacc[...] = jnp.zeros_like(hacc)
    base = s * (rows * ports)

    def use_sources(b, kind):
        cols = pl.ds(pl.multiple_of(b * slice_len + kind * width, LANES), width)
        acc[...] += dot(stack_hi_lo(gath[kind, b]), m2[:, cols], NT)

    def use_records(b):
        values = jnp.concatenate([rec[b, j, :STEPS, :] for j in range(subs - 1)], axis=1)
        keys = jnp.concatenate([rec[b, j, STEPS : STEPS + 1, :] for j in range(subs - 1)], axis=1)
        packed = stack_hi_lo(values)

        def one(r, carry):
            ids = (iota((ports, (subs - 1) * LANES), 0) + (base + r * ports)).astype(F32)
            land = jnp.where(ids == keys, 1.0, 0.0).astype(BF16)
            hacc[r] += dot(packed, land, NT)
            return carry

        lax.fori_loop(0, rows, one, 0)

    def use(b):
        for k in range(CHUNKS):
            use_sources(b, k)
        use_records(b)

    use(me)
    for k in range(CHUNKS + 1):
        line_copy(k, partner, 2, partner).wait_recv()
    use(partner)

    def ring(i, carry):
        below = i % 2 == 0
        k = i // 2 + 1
        zb = jnp.where(below, z - k, z + k)
        zt = jnp.where(below, z + 1, z - 1)
        b = zb * 2 + c

        @pl.when(jnp.logical_and(zb >= 0, zb < zn))
        def _():
            for kind in range(CHUNKS + 1):
                line_copy(kind, b, 0, partner).wait_recv()

                @pl.when(jnp.logical_and(zt >= 0, zt < zn))
                def _():
                    line_copy(kind, b, 0, zt * 2 + c).start()

                line_copy(kind, b, 2, partner).start()
            use(b)
            other = zb * 2 + (1 - c)
            for kind in range(CHUNKS + 1):
                line_copy(kind, other, 2, partner).wait_recv()
            use(other)

        return carry

    lax.fori_loop(0, 2 * (zn - 1), ring, 0)

    tot = acc[...]
    for r in range(rows):
        landed = hacc[r]
        landed = landed[:STEPS] + landed[STEPS:]
        tot = tot - dot(stack_hi_lo(landed), m2[:, r * slice_len : r * slice_len + ports], NT)
    first = four_terms(tot)
    fst[me] = lax.dot_general(first, slot_own, NN, precision=HIGHEST, preferred_element_type=F32)

    def fst_copy(b, at, target):
        return pltpu.make_async_remote_copy(
            src_ref=fst.at[b], dst_ref=fst.at[b], send_sem=fst_send.at[at],
            recv_sem=fst_recv.at[b], device_id=(s, target), device_id_type=MESH,
        )

    for j in range(1, rows):
        fst_copy(me, j - 1, lax.rem(me + j, rows)).start()

    for j in range(1, zn):
        zb = lax.rem(z + j, zn)
        elem_copy(zb * 2 + c, 0, partner).wait_recv()
        elem_copy(zb * 2 + c, zb, partner).start()
    for j in range(zn):
        elem_copy(lax.rem(z + j, zn) * 2 + (1 - c), 0, partner).wait_recv()

    w = elem[...].reshape(total, total)
    self_row = jnp.sum(jnp.where(iota((total, total), 0) == iota((total, total), 1), w, 0.0), axis=0, keepdims=True)
    w_hi, w_lo = hi_lo(jnp.transpose(w))
    wc[:, :total] = w_hi
    wc[:, total:] = w_lo

    full = (8, total)
    is_arrest = iota(full, 1) % elems < arrests
    arrest_gain = jnp.where(is_arrest, jnp.broadcast_to(all_par[1:2, :], full), 0.0)
    core_gain = jnp.where(is_arrest, 0.0, jnp.broadcast_to(all_par[2:3, :], full))
    elem_self = jnp.broadcast_to(self_row, full)
    volts0 = jnp.broadcast_to(all_par[3:4, :], full)
    flux0 = jnp.broadcast_to(all_par[4:5, :], full)

    for j in range(1, rows):
        fst_copy(lax.rem(me + j, rows), j - 1, partner).wait_recv()
    fall[...] = jnp.concatenate(
        [sum(fst[h * group + i] for i in range(group)) for h in range(halves)], axis=1
    )

    def advance(t, carry):
        voltage, flux_now = carry
        first_now = jnp.broadcast_to(fall[pl.ds(t, 1), :], full)
        iterate = voltage
        for newton_pass in range(NEWTON):
            linked = flux_now + half_step * (iterate + voltage)
            ratio = iterate * (1.0 / knee_volts)
            rr = ratio * ratio
            ll = linked * linked
            current = arrest_gain * (iterate * (1.0 + rr)) + core_gain * (linked * (1.0 + cubic_term * ll))
            slope = arrest_gain * (1.0 + 3.0 * rr) + core_gain * (half_step + (half_step * 3.0 * cubic_term) * ll)
            recip = 1.0 / (1.0 + elem_self * slope)
            got = dot(stack_hi_lo(current), wc[...])
            coupled = got[:8, :total] + got[8:, :total] + got[:8, total:]
            iterate = iterate - (iterate - first_now + coupled) * recip
        vo[pl.ds(t, 1), :] = iterate[0:1]
        cu[pl.ds(t, 1), :] = current[0:1]
        return iterate, flux_now + half_step * (iterate + voltage)

    lax.fori_loop(0, STEPS, advance, (volts0, flux0))

    reach = four_terms(dot(stack_hi_lo(cu[...]), x2[...], NT))
    put = jnp.where(jnp.logical_and(at_slot, owner_of == me), 1.0, 0.0)
    placed = lax.dot_general(vo[...], put, NT, precision=HIGHEST, preferred_element_type=F32)
    here = lax.dot_general(jnp.ones((8, total), BF16), put.astype(BF16), NT, preferred_element_type=F32)[0:1]
    stacked = jnp.where(here > 0.5, placed, first - reach)
    out[0] = stacked
    summed = jnp.sum(stacked, axis=0, keepdims=True)
    fout[...] = flux[...] + half_step * (prev[...] + 2.0 * summed - stacked[STEPS - 1 : STEPS])

    for k in range(CHUNKS + 1):
        @pl.when(z + 1 < zn)
        def _():
            line_copy(k, me, 0, partner).wait_send()

        @pl.when(z > 0)
        def _():
            line_copy(k, me, 1, partner).wait_send()

        line_copy(k, me, 2, partner).wait_send()

    def drain(i, carry):
        below = i % 2 == 0
        k = i // 2 + 1
        zb = jnp.where(below, z - k, z + k)
        zt = jnp.where(below, z + 1, z - 1)
        b = zb * 2 + c

        @pl.when(jnp.logical_and(zb >= 0, zb < zn))
        def _():
            for kind in range(CHUNKS + 1):
                @pl.when(jnp.logical_and(zt >= 0, zt < zn))
                def _():
                    line_copy(kind, b, 0, partner).wait_send()

                line_copy(kind, b, 2, partner).wait_send()

        return carry

    lax.fori_loop(0, 2 * (zn - 1), drain, 0)
    for j in range(1, subs):
        pltpu.make_async_remote_copy(
            src_ref=recout, dst_ref=rec.at[me, subs - 1 - j], send_sem=rec_send.at[j - 1],
            recv_sem=rec_recv.at[subs - 1 - j], device_id=(lax.rem(s + j, subs), me), device_id_type=MESH,
        ).wait_send()
    for j in range(1, rows):
        pltpu.make_async_remote_copy(
            src_ref=par.at[me], dst_ref=par.at[me], send_sem=par_send.at[j - 1],
            recv_sem=par_recv.at[me], device_id=(s, partner), device_id_type=MESH,
        ).wait_send()
        fst_copy(me, j - 1, partner).wait_send()
    for j in range(1, zn):
        elem_copy(me, zn + j - 1, partner).wait_send()
    for j in range(zn):
        elem_copy(lax.rem(z + j, zn) * 2 + c, lax.rem(z + j, zn), partner).wait_send()


def on_device(subs, rows, *args):
    inverse, sources = args[0], args[1]
    ports = inverse.shape[1]
    order = inverse.shape[2]
    slice_len = sources.shape[2]
    arrests, cores = args[10].shape[1], args[11].shape[1]
    elems = arrests + cores
    total = rows * elems
    zn = rows // 2
    vmem = pl.BlockSpec(memory_space=pltpu.VMEM)
    hbm = pl.BlockSpec(memory_space=pl.ANY)
    dma = pltpu.SemaphoreType.DMA
    return pl.pallas_call(
        functools.partial(kernel, subs, rows, ports, slice_len, arrests, cores),
        out_shape=(
            jax.ShapeDtypeStruct((1, STEPS, ports), F32),
            jax.ShapeDtypeStruct((1, ports), F32),
        ),
        in_specs=[hbm, hbm] + [vmem] * 10,
        out_specs=(vmem, vmem),
        scratch_shapes=[
            pltpu.VMEM((ports, order), F32),
            pltpu.VMEM((2 * ports, order), BF16),
            pltpu.VMEM((CHUNKS, rows, STEPS, slice_len // CHUNKS), F32),
            pltpu.VMEM((rows, subs - 1, STEPS + 8, LANES), F32),
            pltpu.VMEM((rows, elems, total), F32),
            pltpu.VMEM((rows, 8, LANES), F32),
            pltpu.VMEM((rows, STEPS, LANES), F32),
            pltpu.VMEM((STEPS + 8, LANES), F32),
            pltpu.VMEM((2 * ports, total), BF16),
            pltpu.VMEM((total, 2 * total), BF16),
            pltpu.VMEM((STEPS, total), F32),
            pltpu.VMEM((STEPS, total), F32),
            pltpu.VMEM((STEPS, total), F32),
            pltpu.VMEM((2 * STEPS, 2 * ports), F32),
            pltpu.VMEM((rows, 2 * STEPS, ports), F32),
            dma((rows,)),
            dma((CHUNKS,)),
            dma((CHUNKS + 1, rows, 3)),
            dma((CHUNKS + 1, rows)),
            dma((subs - 1,)),
            dma((subs - 1,)),
            dma((rows - 1,)),
            dma((rows,)),
            dma((2 * zn - 1,)),
            dma((rows,)),
            dma((rows - 1,)),
            dma((rows,)),
        ],
        compiler_params=pltpu.CompilerParams(collective_id=0, has_side_effects=True),
        name="window",
    )(*args)


def solution(mesh):
    subs, rows = mesh.shape["sub"], mesh.shape["row"]
    in_specs = (
        P("sub", "row", None),
        P("sub", None, "row"),
        P("sub", None, "row"),
    ) + (P("sub", "row"),) * 9
    out_specs = (P("sub", None, "row"), P("sub", "row"))
    return jax.shard_map(
        functools.partial(on_device, subs, rows),
        mesh=mesh, in_specs=in_specs, out_specs=out_specs, check_vma=False,
    )
```

time: 158 us -> 42.6 us (0.27)
  blocking collectives: 67.2 us -> 0 us
  Pallas kernels: 0 us -> 39.3 us
  matrix products: 18.1 us -> 0 us
  waiting for transfers between devices: 17.9 us -> 0 us
  local copies, waits for them, and re-layouts: 19.8 us -> 2.43 us
  between operations: 14.9 us -> 0.64 us
  other arithmetic: 9.39 us -> 0 us
  starting transfers between devices: 9.39 us -> 0 us
    all_gather x4 -> x0, blocking collectives: 58.2 us -> none  [the longest x1 15.7 us: on_device(): lax.all_gather(window, 'row', axis=1, tiled=True)]
    pallas_call x0 -> x1, Pallas kernels: none -> 39.3 us  [on_device(): pl.pallas_call(functools.partial(kernel, subs, rows, ports, slice_len, ar...]
    dot_general x37 -> x0, matrix products: 18.1 us -> none  [the longest x32 8.45 us: elem_advance(): jnp.dot(elem_matrix, current, precision=lax.Precision.HIGHEST)]
    reduce_scatter x1 -> x0, waiting for transfers between devices: 13.3 us -> none  [on_device(): lax.psum_scatter(partial_value, 'row', scatter_dimension=1, tiled=True)]
    all_to_all x2 -> x0, starting transfers between devices: 9.39 us -> none  [the longest x1 5.19 us: on_device(): lax.all_to_all(tag_block, 'sub', split_axis=0, concat_axis=0, tiled=True)]
    unnamed x1 -> x0, blocking collectives: 8.92 us -> none
    gather x9 -> x0, local copies, waits for them, and re-layouts: 6.67 us -> none  [the longest x1 1.24 us: on_device(): self_imp = jnp.diagonal(own_block)]
    another operation x2 -> x0, local copies, waits for them, and re-layouts: 6.64 us -> none  [the longest x1 6.62 us: on_device(): matrix.reshape(port_rows, row_count, slice_len)[:, :, :port_rows]]
  transfers between devices with their start and end apart: 3 -> 0, of which waited for: 2 -> 0; matrix products, arithmetic and copies ran while one was open for 12% -> 0% of each run, Pallas kernels for 0% -> 0%
where the time goes in v1:
time: 42.6 us; the launch traced here: 42.4 us
  Pallas kernels  39.3 us (92%)
  local copies, waits for them, and re-layouts  2.43 us (6%)
  between operations  0.64 us (2%)
    pallas_call x1, Pallas kernels, on_device(): pl.pallas_call(functools.partial(kernel, subs, rows, ports, slice_len, ar...  39.3 us
    unnamed x2, local copies, waits for them, and re-layouts  2.43 us

profile of v1, /device:TPU:0, one launch (start us, length us, event | category | flops | bytes accessed | tf_op | source)
XLA Modules:
  0.0 42.4 jit_solution(7091548919824246484)
XLA Ops:
  0.6 39.3 %window.1 = (f32[1,16,128]{2,1,0:T(8,128)}, f32[1,128]{1,0:T(1,128)}) custom-call(f32[1,128,12288]{2,1,0:T(8,128)} %inv.1, f32[1,16,1536]{2,1,0:T(8,128)} %src.1, f32[1,32,128]{2,1,0:T(8,128)} %hist.1, s32[1,128]{1,0:T(1,128)} %dest.1, s32[1,128]{1,0:T(1,128)} %port.1, s32[1,128]{1,0:T(1,128)} %delay.1, f32[1,128]{1,0:T(1,128)} %prev.1, f32[1,128]{1,0:T(1,128)} %flux.1, ...), custom_call_target="tpu_custom_call" | custom-call | tf_op jit(solution)/shard_map/window/pallas_call | solution.py:397
  40.0 1.3 %copy.16 = f32[1,16,128]{2,1,0:T(8,128)} copy(f32[1,16,128]{2,1,0:T(8,128)} %get-tuple-element.4) | data formatting | bytes 16384
  41.3 1.1 %copy.17 = f32[1,128]{1,0:T(1,128)} copy(f32[1,128]{1,0:T(1,128)} %get-tuple-element.5) | data formatting | bytes 1024

commit v2 on v1

v2 whole, which is shorter than its diff:
```python
import functools

import jax
import jax.numpy as jnp
from jax import lax
from jax.experimental import pallas as pl
from jax.experimental.pallas import tpu as pltpu
from jax.sharding import PartitionSpec as P

STEPS = 16
HISTORY = 32
NEWTON = 2
CHUNKS = 2
LANES = 128

half_step = 0.25
knee_volts = 1.5
cubic_term = 0.25

F32 = jnp.float32
BF16 = jnp.bfloat16
MESH = pl.DeviceIdType.MESH
NN = (((1,), (0,)), ((), ()))
NT = (((1,), (1,)), ((), ()))
HIGHEST = lax.Precision.HIGHEST


def iota(shape, axis):
    return lax.broadcasted_iota(jnp.int32, shape, axis)


def hi_lo(x):
    high = x.astype(BF16)
    return high, (x - high.astype(F32)).astype(BF16)


def stack_hi_lo(x):
    return jnp.concatenate(hi_lo(x), axis=0)


def dot(a, b, dims=NN):
    return lax.dot_general(a, b, dims, preferred_element_type=F32)


def four_terms(r):
    n, m = r.shape[0] // 2, r.shape[1] // 2
    return (r[:n, :m] + r[n:, :m]) + (r[:n, m:] + r[n:, m:])


def kernel(
    subs, rows, ports, slice_len, arrests, cores, n_small,
    inv, src, *refs,
):
    small_hbm, refs = refs[:n_small], refs[n_small:]
    out, refs = refs[0], refs[1:]
    small, refs = refs[:n_small], refs[n_small:]
    (
        m32, mp32, mp2, gath, recin, rec, elem, par, fst, recout, x2, wc, fall, vo, cu, acc, hacc,
        small_sem, inv_sem, mp_sem, src_sem, line_send, line_recv, sub_send, sub_recv,
        rec_send, rec_recv, par_send, par_recv, elem_send, elem_recv, fst_send, fst_recv,
    ) = refs
    hist, dest, port, delay, prev, flux, again, cgain, aslots, cslots = small
    s = lax.axis_index("sub")
    me = lax.axis_index("row")
    z, c = me // 2, me % 2
    zn = rows // 2
    partner = z * 2 + (1 - c)
    elems = arrests + cores
    group = LANES // elems
    total = rows * elems
    halves = total // LANES
    width = slice_len // CHUNKS
    peers = subs - 1
    turns = 2 * (zn - 1)

    barrier = pltpu.get_barrier_semaphore()
    for j in range(1, rows):
        pl.semaphore_signal(barrier, inc=1, device_id=(s, lax.rem(me + j, rows)), device_id_type=MESH)
    for j in range(1, subs):
        pl.semaphore_signal(barrier, inc=1, device_id=(lax.rem(s + j, subs), me), device_id_type=MESH)

    small_copies = [
        pltpu.make_async_copy(small_hbm[i], small[i], small_sem.at[i]) for i in range(n_small)
    ]
    for copy in small_copies:
        copy.start()

    def src_copy(k):
        return pltpu.make_async_copy(
            src.at[0, :, pl.ds(k * width, width)], gath.at[k, me], src_sem.at[k]
        )

    for k in range(CHUNKS):
        src_copy(k).start()

    def mp_copy(r):
        return pltpu.make_async_copy(
            inv.at[0, :, pl.ds(r * slice_len, ports)], mp32.at[:, pl.ds(r * ports, ports)], mp_sem.at[r]
        )

    for r in range(rows):
        mp_copy(r).start()

    def inv_copy(b):
        cols = pl.ds(pl.multiple_of(b * slice_len, LANES), slice_len)
        return pltpu.make_async_copy(inv.at[0, :, cols], m32.at[:, cols], inv_sem.at[b])

    steps_z = [0]
    for j in range(1, zn):
        hop = (j + 1) // 2
        steps_z.append(hop if j % 2 == 1 else zn - hop)
    for hop in steps_z:
        zb = lax.rem(z + hop, zn)
        inv_copy(zb * 2 + c).start()
        inv_copy(zb * 2 + (1 - c)).start()

    for copy in small_copies:
        copy.wait()

    shifted = hist[0]
    shift = HISTORY - delay[...]
    bit = 1
    while bit <= HISTORY - STEPS:
        moved = pltpu.roll(shifted, HISTORY - bit, 0)
        shifted = jnp.where((shift // bit) % 2 == 1, moved, shifted)
        bit *= 2
    recout[:STEPS, :] = shifted[:STEPS, :]
    k8 = iota((8, LANES), 0)
    tags = jnp.where(k8 == 0, dest[...], jnp.where(k8 == 1, port[...] // ports, port[...] % ports))
    recout[STEPS:, :] = tags.astype(F32)

    lane16a, row16a = iota((arrests, LANES), 1), iota((arrests, LANES), 0)
    lane16c, row16c = iota((cores, LANES), 1), iota((cores, LANES), 0)
    put_a = jnp.where(lane16a % elems == row16a, 1.0, 0.0).astype(BF16)
    put_c = jnp.where(lane16c % elems == row16c + arrests, 1.0, 0.0).astype(BF16)
    slot_a = jnp.broadcast_to(aslots[...].astype(F32), (8, arrests)).astype(BF16)
    slot_c = jnp.broadcast_to(cslots[...].astype(F32), (8, cores)).astype(BF16)
    slot_row = (dot(slot_a, put_a) + dot(slot_c, put_c))[0:1, :]
    hit = iota((ports, LANES), 0).astype(F32) == slot_row
    slot_tiled = jnp.where(hit, 1.0, 0.0)
    slot_own = jnp.where(iota((ports, LANES), 1) // elems == me % group, slot_tiled, 0.0)
    r8 = iota((8, ports), 0)
    params = jnp.where(
        r8 == 0,
        iota((8, ports), 1).astype(F32),
        jnp.where(
            r8 == 1,
            again[...],
            jnp.where(r8 == 2, cgain[...], jnp.where(r8 == 3, prev[...], flux[...])),
        ),
    )
    par[me] = lax.dot_general(params, slot_own, NN, precision=HIGHEST, preferred_element_type=F32)

    for k in range(CHUNKS):
        src_copy(k).wait()
    pl.semaphore_wait(barrier, rows + subs - 2)

    def remote(ref_from, ref_to, send, recv, to_sub, to_row):
        return pltpu.make_async_remote_copy(
            src_ref=ref_from, dst_ref=ref_to, send_sem=send, recv_sem=recv,
            device_id=(to_sub, to_row), device_id_type=MESH,
        )

    def sub_copy(j):
        return remote(
            recout, recin.at[peers - j], sub_send.at[j - 1], sub_recv.at[peers - j],
            lax.rem(s + j, subs), me,
        )

    def par_copy(b, at, target):
        return remote(par.at[b], par.at[b], par_send.at[at], par_recv.at[b], s, target)

    def line_copy(kind, b, way, target):
        ref = gath.at[kind, b]
        return remote(ref, ref, line_send.at[kind, b, way], line_recv.at[kind, b], s, target)

    def rec_copy(b, at, target):
        return remote(rec.at[b], rec.at[b], rec_send.at[at], rec_recv.at[b], s, target)

    def elem_copy(b, at, target):
        return remote(elem.at[b], elem.at[b], elem_send.at[at], elem_recv.at[b], s, target)

    def fst_copy(b, at, target):
        return remote(fst.at[b], fst.at[b], fst_send.at[at], fst_recv.at[b], s, target)

    for j in range(1, subs):
        sub_copy(j).start()
    for j in range(1, rows):
        par_copy(me, j - 1, lax.rem(me + j, rows)).start()
    for k in range(CHUNKS):
        @pl.when(z + 1 < zn)
        def _():
            line_copy(k, me, 0, me + 2).start()

        @pl.when(z > 0)
        def _():
            line_copy(k, me, 1, me - 2).start()

        line_copy(k, me, 2, partner).start()

    for r in range(rows):
        mp_copy(r).wait()
    mp_hi, mp_lo = hi_lo(mp32[...])
    mp2[:ports, :] = mp_hi
    mp2[ports:, :] = mp_lo
    acc[...] = jnp.zeros_like(acc)
    hacc[...] = jnp.zeros_like(hacc)

    for j in range(1, subs):
        sub_copy(j).wait_recv()
    for j in range(peers):
        rec[me, j * STEPS : (j + 1) * STEPS, :] = recin[j, :STEPS, :]
    named = [
        jnp.where(
            recin[j, STEPS : STEPS + 1, :] == s.astype(F32), recin[j, STEPS + 1 : STEPS + 2, :], -1.0
        )
        for j in range(peers)
    ]
    spots = [recin[j, STEPS + 2 : STEPS + 3, :] for j in range(peers)]
    for j, row in enumerate(named + spots):
        rec[me, peers * STEPS + j : peers * STEPS + j + 1, :] = row
    for j in range(1, zn):
        rec_copy(me, zn + j - 1, lax.rem(z + j, zn) * 2 + c).start()
    rec_copy(me, z, partner).start()

    def turn(i):
        below = i % 2 == 0
        k = i // 2 + 1
        zb = jnp.where(below, z - k, z + k)
        zt = jnp.where(below, z + 1, z - 1)
        return zb, zt, jnp.logical_and(zb >= 0, zb < zn), jnp.logical_and(zt >= 0, zt < zn)

    def forward(i, carry):
        zb, zt, valid, onward = turn(i)
        b = zb * 2 + c

        @pl.when(valid)
        def _():
            for kind in range(CHUNKS):
                line_copy(kind, b, 0, partner).wait_recv()

                @pl.when(onward)
                def _():
                    line_copy(kind, b, 0, zt * 2 + c).start()

                line_copy(kind, b, 2, partner).start()

        return carry

    lax.fori_loop(0, 2, forward, 0)

    for j in range(1, rows):
        par_copy(lax.rem(me + j, rows), j - 1, partner).wait_recv()
    all_par = jnp.concatenate(
        [sum(par[h * group + i] for i in range(group)) for h in range(halves)], axis=1
    )
    slots_all = all_par[0:1, :]
    at_slot = iota((ports, total), 0).astype(F32) == slots_all
    owner_of = iota((ports, total), 1) // elems
    pick = None
    for r in range(rows):
        choose = jnp.where(jnp.logical_and(at_slot, owner_of == r), 1.0, 0.0).astype(BF16)
        term = dot(mp2[:, r * ports : (r + 1) * ports], choose)
        pick = term if pick is None else pick + term
    x2[...] = pick.astype(BF16)
    slot_cols = jnp.transpose(slot_tiled)[:elems].astype(BF16)
    elem[me] = dot(slot_cols, x2[:ports, :]) + dot(slot_cols, x2[ports:, :])
    for j in range(1, zn):
        elem_copy(me, zn + j - 1, lax.rem(z + j, zn) * 2 + c).start()
    elem_copy(me, z, partner).start()

    def use_sources(b):
        inv_copy(b).wait()
        for kind in range(CHUNKS):
            cols = pl.ds(pl.multiple_of(b * slice_len + kind * width, LANES), width)
            acc[...] += dot(stack_hi_lo(gath[kind, b]), stack_hi_lo(m32[:, cols]), NT)

    def use_records(b):
        values = jnp.concatenate([rec[b, j * STEPS : (j + 1) * STEPS, :] for j in range(peers)], axis=1)
        tag = rec[b, peers * STEPS :, :]
        owner = jnp.concatenate([tag[j : j + 1, :] for j in range(peers)], axis=1)
        spot = jnp.concatenate([tag[peers + j : peers + j + 1, :] for j in range(peers)], axis=1)
        land = jnp.where(iota((ports, peers * LANES), 0).astype(F32) == spot, 1.0, 0.0).astype(BF16)
        split = jnp.concatenate([jnp.where(owner == float(r), values, 0.0) for r in range(rows)], axis=0)
        hacc[...] += dot(stack_hi_lo(split), land, NT)

    use_records(me)
    use_sources(me)
    for k in range(CHUNKS):
        line_copy(k, partner, 2, partner).wait_recv()
    use_sources(partner)

    def consume(i):
        zb, zt, valid, onward = turn(i)

        @pl.when(valid)
        def _():
            use_sources(zb * 2 + c)
            other = zb * 2 + (1 - c)
            for kind in range(CHUNKS):
                line_copy(kind, other, 2, partner).wait_recv()
            use_sources(other)

    def ring(i, carry):
        forward(i + 2, 0)
        consume(i)
        return carry

    lax.fori_loop(0, turns - 2, ring, 0)

    def pass_on(j, carry):
        zb = lax.rem(z + j, zn)
        b = zb * 2 + c
        rec_copy(b, 0, partner).wait_recv()
        rec_copy(b, zb, partner).start()
        use_records(b)
        return carry

    lax.fori_loop(1, zn, pass_on, 0)
    for j in range(1, zn):
        zb = lax.rem(z + j, zn)
        elem_copy(zb * 2 + c, 0, partner).wait_recv()
        elem_copy(zb * 2 + c, zb, partner).start()

    def last(i, carry):
        consume(i)
        return carry

    lax.fori_loop(turns - 2, turns, last, 0)

    def take(j, carry):
        b = lax.rem(z + j, zn) * 2 + (1 - c)
        rec_copy(b, 0, partner).wait_recv()
        use_records(b)
        return carry

    lax.fori_loop(0, zn, take, 0)

    landed = hacc[: rows * STEPS, :] + hacc[rows * STEPS :, :]
    landed = jnp.concatenate([landed[r * STEPS : (r + 1) * STEPS, :] for r in range(rows)], axis=1)
    first = four_terms(acc[...] - dot(stack_hi_lo(landed), mp2[...], NT))
    mine = dot(stack_hi_lo(first), slot_own.astype(BF16))
    fst[me] = mine[:STEPS] + mine[STEPS:]
    for j in range(1, rows):
        fst_copy(me, j - 1, lax.rem(me + j, rows)).start()

    for j in range(zn):
        elem_copy(lax.rem(z + j, zn) * 2 + (1 - c), 0, partner).wait_recv()

    w = elem[...].reshape(total, total)
    self_row = jnp.sum(jnp.where(iota((total, total), 0) == iota((total, total), 1), w, 0.0), axis=0, keepdims=True)
    w_hi, w_lo = hi_lo(jnp.transpose(w))
    wc[:, :total] = w_hi
    wc[:, total:] = w_lo

    full = (8, total)
    is_arrest = iota(full, 1) % elems < arrests
    arrest_gain = jnp.where(is_arrest, jnp.broadcast_to(all_par[1:2, :], full), 0.0)
    core_gain = jnp.where(is_arrest, 0.0, jnp.broadcast_to(all_par[2:3, :], full))
    elem_self = jnp.broadcast_to(self_row, full)
    volts0 = jnp.broadcast_to(all_par[3:4, :], full)
    flux0 = jnp.broadcast_to(all_par[4:5, :], full)
    put = jnp.where(jnp.logical_and(at_slot, owner_of == me), 1.0, 0.0).astype(BF16)
    here = dot(jnp.ones((8, total), BF16), put, NT)[0:1]

    for j in range(1, subs):
        sub_copy(j).wait_send()
    for k in range(CHUNKS):
        @pl.when(z + 1 < zn)
        def _():
            line_copy(k, me, 0, partner).wait_send()

        @pl.when(z > 0)
        def _():
            line_copy(k, me, 1, partner).wait_send()

        line_copy(k, me, 2, partner).wait_send()

    def drain(i, carry):
        zb, zt, valid, onward = turn(i)
        b = zb * 2 + c

        @pl.when(valid)
        def _():
            for kind in range(CHUNKS):
                @pl.when(onward)
                def _():
                    line_copy(kind, b, 0, partner).wait_send()

                line_copy(kind, b, 2, partner).wait_send()

        return carry

    lax.fori_loop(0, turns, drain, 0)
    for j in range(1, rows):
        par_copy(me, j - 1, partner).wait_send()
    for at in range(2 * zn - 1):
        rec_copy(me, at, partner).wait_send()
        elem_copy(me, at, partner).wait_send()

    for j in range(1, rows):
        fst_copy(lax.rem(me + j, rows), j - 1, partner).wait_recv()
    fall[...] = jnp.concatenate(
        [sum(fst[h * group + i] for i in range(group)) for h in range(halves)], axis=1
    )

    def advance(t, carry):
        voltage, flux_now = carry
        first_now = jnp.broadcast_to(fall[pl.ds(t, 1), :], full)
        iterate = voltage
        for newton_pass in range(NEWTON):
            linked = flux_now + half_step * (iterate + voltage)
            ratio = iterate * (1.0 / knee_volts)
            rr = ratio * ratio
            ll = linked * linked
            current = arrest_gain * (iterate * (1.0 + rr)) + core_gain * (linked * (1.0 + cubic_term * ll))
            slope = arrest_gain * (1.0 + 3.0 * rr) + core_gain * (half_step + (half_step * 3.0 * cubic_term) * ll)
            recip = 1.0 / (1.0 + elem_self * slope)
            got = dot(stack_hi_lo(current), wc[...])
            coupled = got[:8, :total] + got[8:, :total] + got[:8, total:]
            iterate = iterate - (iterate - first_now + coupled) * recip
        vo[pl.ds(t, 1), :] = iterate[0:1]
        cu[pl.ds(t, 1), :] = current[0:1]
        return iterate, flux_now + half_step * (iterate + voltage)

    lax.fori_loop(0, STEPS, advance, (volts0, flux0))

    reach = four_terms(dot(stack_hi_lo(cu[...]), x2[...], NT))
    placed = dot(stack_hi_lo(vo[...]), put, NT)
    stacked = jnp.where(here > 0.5, placed[:STEPS] + placed[STEPS:], first - reach)
    out[:STEPS, :] = stacked
    summed = jnp.sum(stacked, axis=0, keepdims=True)
    last_flux = flux[...] + half_step * (prev[...] + 2.0 * summed - stacked[STEPS - 1 : STEPS])
    out[STEPS:, :] = jnp.broadcast_to(last_flux, (8, ports))
    for j in range(1, rows):
        fst_copy(me, j - 1, partner).wait_send()


def on_device(subs, rows, *args):
    inverse, sources = args[0], args[1]
    ports = inverse.shape[1]
    order = inverse.shape[2]
    slice_len = sources.shape[2]
    arrests, cores = args[10].shape[1], args[11].shape[1]
    elems = arrests + cores
    total = rows * elems
    zn = rows // 2
    tag_rows = -(-2 * (subs - 1) // 8) * 8
    vmem = pl.BlockSpec(memory_space=pltpu.VMEM)
    hbm = pl.BlockSpec(memory_space=pl.ANY)
    dma = pltpu.SemaphoreType.DMA
    small = args[2:]
    both = pl.pallas_call(
        functools.partial(kernel, subs, rows, ports, slice_len, arrests, cores, len(small)),
        out_shape=jax.ShapeDtypeStruct((STEPS + 8, ports), F32),
        in_specs=[hbm] * len(args),
        out_specs=vmem,
        scratch_shapes=[pltpu.VMEM(a.shape, a.dtype) for a in small]
        + [
            pltpu.VMEM((ports, order), F32),
            pltpu.VMEM((ports, rows * ports), F32),
            pltpu.VMEM((2 * ports, rows * ports), BF16),
            pltpu.VMEM((CHUNKS, rows, STEPS, slice_len // CHUNKS), F32),
            pltpu.VMEM((subs - 1, STEPS + 8, LANES), F32),
            pltpu.VMEM((rows, (subs - 1) * STEPS + tag_rows, LANES), F32),
            pltpu.VMEM((rows, elems, total), F32),
            pltpu.VMEM((rows, 8, LANES), F32),
            pltpu.VMEM((rows, STEPS, LANES), F32),
            pltpu.VMEM((STEPS + 8, LANES), F32),
            pltpu.VMEM((2 * ports, total), BF16),
            pltpu.VMEM((total, 2 * total), BF16),
            pltpu.VMEM((STEPS, total), F32),
            pltpu.VMEM((STEPS, total), F32),
            pltpu.VMEM((STEPS, total), F32),
            pltpu.VMEM((2 * STEPS, 2 * ports), F32),
            pltpu.VMEM((2 * STEPS * rows, ports), F32),
            dma((len(small),)),
            dma((rows,)),
            dma((rows,)),
            dma((CHUNKS,)),
            dma((CHUNKS, rows, 3)),
            dma((CHUNKS, rows)),
            dma((subs - 1,)),
            dma((subs - 1,)),
            dma((2 * zn - 1,)),
            dma((rows,)),
            dma((rows - 1,)),
            dma((rows,)),
            dma((2 * zn - 1,)),
            dma((rows,)),
            dma((rows - 1,)),
            dma((rows,)),
        ],
        compiler_params=pltpu.CompilerParams(collective_id=0, has_side_effects=True),
        name="window",
    )(*args)
    return both[None, :STEPS], both[STEPS : STEPS + 1]


def solution(mesh):
    subs, rows = mesh.shape["sub"], mesh.shape["row"]
    in_specs = (
        P("sub", "row", None),
        P("sub", None, "row"),
        P("sub", None, "row"),
    ) + (P("sub", "row"),) * 9
    out_specs = (P("sub", None, "row"), P("sub", "row"))
    return jax.shard_map(
        functools.partial(on_device, subs, rows),
        mesh=mesh, in_specs=in_specs, out_specs=out_specs, check_vma=False,
    )
```

time: 42.6 us -> 38.1 us (0.89)
  Pallas kernels: 39.3 us -> 34.7 us
    pallas_call x1, Pallas kernels: 39.3 us -> 34.7 us  [on_device(): pl.pallas_call(functools.partial(kernel, subs, rows, ports, slice_len, ar...]
    unnamed x2 -> x0, local copies, waits for them, and re-layouts: 2.43 us -> none
    broadcast_in_dim x0 -> x1, local copies, waits for them, and re-layouts: none -> 1.29 us  [on_device(): return (both[None, :STEPS], both[STEPS:STEPS + 1])]
    slice x0 -> x1, local copies, waits for them, and re-layouts: none -> 1.19 us  [on_device(): return (both[None, :STEPS], both[STEPS:STEPS + 1])]
where the time goes in v2:
time: 38.1 us; the launch traced here: 37.8 us
  Pallas kernels  34.7 us (91%)
  local copies, waits for them, and re-layouts  2.48 us (7%)
  between operations  0.64 us (2%)
    pallas_call x1, Pallas kernels, on_device(): pl.pallas_call(functools.partial(kernel, subs, rows, ports, slice_len, ar...  34.7 us
    broadcast_in_dim x1, local copies, waits for them, and re-layouts, on_device(): return (both[None, :STEPS], both[STEPS:STEPS + 1])  1.29 us
    slice x1, local copies, waits for them, and re-layouts, on_device(): return (both[None, :STEPS], both[STEPS:STEPS + 1])  1.19 us

profile of v2, /device:TPU:0, one launch (start us, length us, event | category | flops | bytes accessed | tf_op | source)
XLA Modules:
  0.0 37.8 jit_solution(9756700874402598256)
XLA Ops:
  0.6 34.7 %window.1 = f32[24,128]{1,0:T(8,128)} custom-call(f32[1,128,12288]{2,1,0:T(8,128)} %inv.1, f32[1,16,1536]{2,1,0:T(8,128)} %src.1, f32[1,32,128]{2,1,0:T(8,128)} %refs_0_.1, s32[1,128]{1,0:T(1,128)} %refs_1_.1, s32[1,128]{1,0:T(1,128)} %refs_2_.1, s32[1,128]{1,0:T(1,128)} %refs_3_.1, f32[1,128]{1,0:T(1,128)} %refs_4_.1, f32[1,128]{1,0:T(1,128)} %refs_5_.1, ...), custom_call_target="tpu_custom_call" | custom-call | tf_op jit(solution)/shard_map/window/pallas_call | solution.py:453
  35.3 1.2 %slice.7 = f32[1,128]{1,0:T(1,128)} slice(f32[24,128]{1,0:T(8,128)} %window.1), slice={[16:17], [0:128]} | slice | bytes 1024 | tf_op jit(solution)/shard_map/slice | solution.py:497
  36.5 1.3 %slice_bitcast_fusion = f32[1,16,128]{2,1,0:T(8,128)} fusion(f32[24,128]{1,0:T(8,128)} %window.1), kind=kLoop, calls=%fused_computation | loop fusion | bytes 16384 | tf_op jit(solution)/shard_map/broadcast_in_dim | solution.py:497

commit v3 on v2

--- a/solution.py
+++ b/solution.py
@@ -55,7 +55,7 @@
     out, refs = refs[0], refs[1:]
     small, refs = refs[:n_small], refs[n_small:]
     (
-        m32, mp32, mp2, gath, recin, rec, elem, par, fst, recout, x2, wc, fall, vo, cu, acc, hacc,
+        m32, m2, mp32, mp2, gath, recin, rec, elem, par, fst, recout, x2, wc, fall, vo, cu, acc, hacc,
         small_sem, inv_sem, mp_sem, src_sem, line_send, line_recv, sub_send, sub_recv,
         rec_send, rec_recv, par_send, par_recv, elem_send, elem_recv, fst_send, fst_recv,
     ) = refs
@@ -151,53 +151,6 @@
     )
     par[me] = lax.dot_general(params, slot_own, NN, precision=HIGHEST, preferred_element_type=F32)
 
-    for k in range(CHUNKS):
-        src_copy(k).wait()
-    pl.semaphore_wait(barrier, rows + subs - 2)
-
-    def remote(ref_from, ref_to, send, recv, to_sub, to_row):
-        return pltpu.make_async_remote_copy(
-            src_ref=ref_from, dst_ref=ref_to, send_sem=send, recv_sem=recv,
-            device_id=(to_sub, to_row), device_id_type=MESH,
-        )
-
-    def sub_copy(j):
-        return remote(
-            recout, recin.at[peers - j], sub_send.at[j - 1], sub_recv.at[peers - j],
-            lax.rem(s + j, subs), me,
-        )
-
-    def par_copy(b, at, target):
-        return remote(par.at[b], par.at[b], par_send.at[at], par_recv.at[b], s, target)
-
-    def line_copy(kind, b, way, target):
-        ref = gath.at[kind, b]
-        return remote(ref, ref, line_send.at[kind, b, way], line_recv.at[kind, b], s, target)
-
-    def rec_copy(b, at, target):
-        return remote(rec.at[b], rec.at[b], rec_send.at[at], rec_recv.at[b], s, target)
-
-    def elem_copy(b, at, target):
-        return remote(elem.at[b], elem.at[b], elem_send.at[at], elem_recv.at[b], s, target)
-
-    def fst_copy(b, at, target):
-        return remote(fst.at[b], fst.at[b], fst_send.at[at], fst_recv.at[b], s, target)
-
-    for j in range(1, subs):
-        sub_copy(j).start()
-    for j in range(1, rows):
-        par_copy(me, j - 1, lax.rem(me + j, rows)).start()
-    for k in range(CHUNKS):
-        @pl.when(z + 1 < zn)
-        def _():
-            line_copy(k, me, 0, me + 2).start()
-
-        @pl.when(z > 0)
-        def _():
-            line_copy(k, me, 1, me - 2).start()
-
-        line_copy(k, me, 2, partner).start()
-
     for r in range(rows):
         mp_copy(r).wait()
     mp_hi, mp_lo = hi_lo(mp32[...])
@@ -205,6 +158,69 @@
     mp2[ports:, :] = mp_lo
     acc[...] = jnp.zeros_like(acc)
     hacc[...] = jnp.zeros_like(hacc)
+
+    def split_block(j, carry):
+        b = lax.rem(me + j, rows)
+        inv_copy(b).wait()
+        cols = pl.ds(pl.multiple_of(b * slice_len, LANES), slice_len)
+        high, low = hi_lo(m32[:, cols])
+        m2[:ports, cols] = high
+        m2[ports:, cols] = low
+        return carry
+
+    def use_sources(b):
+        for kind in range(CHUNKS):
+            cols = pl.ds(pl.multiple_of(b * slice_len + kind * width, LANES), width)
+            acc[...] += dot(stack_hi_lo(gath[kind, b]), m2[:, cols], NT)
+
+    lax.fori_loop(0, rows, split_block, 0)
+    for k in range(CHUNKS):
+        src_copy(k).wait()
+    use_sources(me)
+    pl.semaphore_wait(barrier, rows + subs - 2)
+
+    def remote(ref_from, ref_to, send, recv, to_sub, to_row):
+        return pltpu.make_async_remote_copy(
+            src_ref=ref_from, dst_ref=ref_to, send_sem=send, recv_sem=recv,
+            device_id=(to_sub, to_row), device_id_type=MESH,
+        )
+
+    def sub_copy(j):
+        return remote(
+            recout, recin.at[peers - j], sub_send.at[j - 1], sub_recv.at[peers - j],
+            lax.rem(s + j, subs), me,
+        )
+
+    def par_copy(b, at, target):
+        return remote(par.at[b], par.at[b], par_send.at[at], par_recv.at[b], s, target)
+
+    def line_copy(kind, b, way, target):
+        ref = gath.at[kind, b]
+        return remote(ref, ref, line_send.at[kind, b, way], line_recv.at[kind, b], s, target)
+
+    def rec_copy(b, at, target):
+        return remote(rec.at[b], rec.at[b], rec_send.at[at], rec_recv.at[b], s, target)
+
+    def elem_copy(b, at, target):
+        return remote(elem.at[b], elem.at[b], elem_send.at[at], elem_recv.at[b], s, target)
+
+    def fst_copy(b, at, target):
+        return remote(fst.at[b], fst.at[b], fst_send.at[at], fst_recv.at[b], s, target)
+
+    for j in range(1, subs):
+        sub_copy(j).start()
+    for j in range(1, rows):
+        par_copy(me, j - 1, lax.rem(me + j, rows)).start()
+    for k in range(CHUNKS):
+        @pl.when(z + 1 < zn)
+        def _():
+            line_copy(k, me, 0, me + 2).start()
+
+        @pl.when(z > 0)
+        def _():
+            line_copy(k, me, 1, me - 2).start()
+
+        line_copy(k, me, 2, partner).start()
 
     for j in range(1, subs):
         sub_copy(j).wait_recv()
@@ -248,6 +264,39 @@
         return carry
 
     lax.fori_loop(0, 2, forward, 0)
+
+    def use_records(b):
+        values = jnp.concatenate([rec[b, j * STEPS : (j + 1) * STEPS, :] for j in range(peers)], axis=1)
+        tag = rec[b, peers * STEPS :, :]
+        owner = jnp.concatenate([tag[j : j + 1, :] for j in range(peers)], axis=1)
+        spot = jnp.concatenate([tag[peers + j : peers + j + 1, :] for j in range(peers)], axis=1)
+        land = jnp.where(iota((ports, peers * LANES), 0).astype(F32) == spot, 1.0, 0.0).astype(BF16)
+        split = jnp.concatenate([jnp.where(owner == float(r), values, 0.0) for r in range(rows)], axis=0)
+        hacc[...] += dot(stack_hi_lo(split), land, NT)
+
+    use_records(me)
+    for k in range(CHUNKS):
+        line_copy(k, partner, 2, partner).wait_recv()
+    use_sources(partner)
+
+    def consume(i):
+        zb, zt, valid, onward = turn(i)
+
+        @pl.when(valid)
+        def _():
+            use_sources(zb * 2 + c)
+            other = zb * 2 + (1 - c)
+            for kind in range(CHUNKS):
+                line_copy(kind, other, 2, partner).wait_recv()
+            use_sources(other)
+
+    def ring(i, carry):
+        forward(i + 2, 0)
+        consume(i)
+        return carry
+
+    early = min(2, turns - 2)
+    lax.fori_loop(0, early, ring, 0)
 
     for j in range(1, rows):
         par_copy(lax.rem(me + j, rows), j - 1, partner).wait_recv()
@@ -269,44 +318,7 @@
         elem_copy(me, zn + j - 1, lax.rem(z + j, zn) * 2 + c).start()
     elem_copy(me, z, partner).start()
 
-    def use_sources(b):
-        inv_copy(b).wait()
-        for kind in range(CHUNKS):
-            cols = pl.ds(pl.multiple_of(b * slice_len + kind * width, LANES), width)
-            acc[...] += dot(stack_hi_lo(gath[kind, b]), stack_hi_lo(m32[:, cols]), NT)
-
-    def use_records(b):
-        values = jnp.concatenate([rec[b, j * STEPS : (j + 1) * STEPS, :] for j in range(peers)], axis=1)
-        tag = rec[b, peers * STEPS :, :]
-        owner = jnp.concatenate([tag[j : j + 1, :] for j in range(peers)], axis=1)
-        spot = jnp.concatenate([tag[peers + j : peers + j + 1, :] for j in range(peers)], axis=1)
-        land = jnp.where(iota((ports, peers * LANES), 0).astype(F32) == spot, 1.0, 0.0).astype(BF16)
-        split = jnp.concatenate([jnp.where(owner == float(r), values, 0.0) for r in range(rows)], axis=0)
-        hacc[...] += dot(stack_hi_lo(split), land, NT)
-
-    use_records(me)
-    use_sources(me)
-    for k in range(CHUNKS):
-        line_copy(k, partner, 2, partner).wait_recv()
-    use_sources(partner)
-
-    def consume(i):
-        zb, zt, valid, onward = turn(i)
-
-        @pl.when(valid)
-        def _():
-            use_sources(zb * 2 + c)
-            other = zb * 2 + (1 - c)
-            for kind in range(CHUNKS):
-                line_copy(kind, other, 2, partner).wait_recv()
-            use_sources(other)
-
-    def ring(i, carry):
-        forward(i + 2, 0)
-        consume(i)
-        return carry
-
-    lax.fori_loop(0, turns - 2, ring, 0)
+    lax.fori_loop(early, turns - 2, ring, 0)
 
     def pass_on(j, carry):
         zb = lax.rem(z + j, zn)
@@ -317,16 +329,6 @@
         return carry
 
     lax.fori_loop(1, zn, pass_on, 0)
-    for j in range(1, zn):
-        zb = lax.rem(z + j, zn)
-        elem_copy(zb * 2 + c, 0, partner).wait_recv()
-        elem_copy(zb * 2 + c, zb, partner).start()
-
-    def last(i, carry):
-        consume(i)
-        return carry
-
-    lax.fori_loop(turns - 2, turns, last, 0)
 
     def take(j, carry):
         b = lax.rem(z + j, zn) * 2 + (1 - c)
@@ -335,6 +337,12 @@
         return carry
 
     lax.fori_loop(0, zn, take, 0)
+
+    def last(i, carry):
+        consume(i)
+        return carry
+
+    lax.fori_loop(turns - 2, turns, last, 0)
 
     landed = hacc[: rows * STEPS, :] + hacc[rows * STEPS :, :]
     landed = jnp.concatenate([landed[r * STEPS : (r + 1) * STEPS, :] for r in range(rows)], axis=1)
@@ -344,6 +352,10 @@
     for j in range(1, rows):
         fst_copy(me, j - 1, lax.rem(me + j, rows)).start()
 
+    for j in range(1, zn):
+        zb = lax.rem(z + j, zn)
+        elem_copy(zb * 2 + c, 0, partner).wait_recv()
+        elem_copy(zb * 2 + c, zb, partner).start()
     for j in range(zn):
         elem_copy(lax.rem(z + j, zn) * 2 + (1 - c), 0, partner).wait_recv()
 
@@ -434,6 +446,11 @@
     out[STEPS:, :] = jnp.broadcast_to(last_flux, (8, ports))
     for j in range(1, rows):
         fst_copy(me, j - 1, partner).wait_send()
+
+
+def give(both, volts, last_flux):
+    volts[0] = both[:STEPS, :]
+    last_flux[...] = both[STEPS : STEPS + 1, :]
 
 
 def on_device(subs, rows, *args):
@@ -458,6 +475,7 @@
         scratch_shapes=[pltpu.VMEM(a.shape, a.dtype) for a in small]
         + [
             pltpu.VMEM((ports, order), F32),
+            pltpu.VMEM((2 * ports, order), BF16),
             pltpu.VMEM((ports, rows * ports), F32),
             pltpu.VMEM((2 * ports, rows * ports), BF16),
             pltpu.VMEM((CHUNKS, rows, STEPS, slice_len // CHUNKS), F32),
@@ -494,7 +512,16 @@
         compiler_params=pltpu.CompilerParams(collective_id=0, has_side_effects=True),
         name="window",
     )(*args)
-    return both[None, :STEPS], both[STEPS : STEPS + 1]
+    return pl.pallas_call(
+        give,
+        out_shape=(
+            jax.ShapeDtypeStruct((1, STEPS, ports), F32),
+            jax.ShapeDtypeStruct((1, ports), F32),
+        ),
+        in_specs=[vmem],
+        out_specs=(vmem, vmem),
+        name="give",
+    )(both)
 
 
 def solution(mesh):

time: 38.1 us -> 36.7 us (0.963)
  local copies, waits for them, and re-layouts: 2.48 us -> 0 us
  Pallas kernels: 34.7 us -> 35.7 us
    pallas_call x0 -> x1, Pallas kernels: none -> 1.31 us  [on_device(): pl.pallas_call(give, out_shape=(jax.ShapeDtypeStruct((1, STEPS, ports), F...]
    broadcast_in_dim x1 -> x0, local copies, waits for them, and re-layouts: 1.29 us -> none  [on_device(): return (both[None, :STEPS], both[STEPS:STEPS + 1])]
    slice x1 -> x0, local copies, waits for them, and re-layouts: 1.19 us -> none  [on_device(): return (both[None, :STEPS], both[STEPS:STEPS + 1])]
where the time goes in v3:
time: 36.7 us; the launch traced here: 36.4 us
  Pallas kernels  35.7 us (97%)
  between operations  0.64 us (2%)
    pallas_call x1, Pallas kernels, on_device(): pl.pallas_call(functools.partial(kernel, subs, rows, ports, slice_len, ar...  34.4 us
    pallas_call x1, Pallas kernels, on_device(): pl.pallas_call(give, out_shape=(jax.ShapeDtypeStruct((1, STEPS, ports), F...  1.31 us

profile of v3, /device:TPU:0, one launch (start us, length us, event | category | flops | bytes accessed | tf_op | source)
XLA Modules:
  0.0 36.4 jit_solution(16669316577333403975)
XLA Ops:
  0.6 34.4 %window.1.both = f32[24,128]{1,0:T(8,128)} custom-call(f32[1,128,12288]{2,1,0:T(8,128)} %inv.1, f32[1,16,1536]{2,1,0:T(8,128)} %src.1, f32[1,32,128]{2,1,0:T(8,128)} %refs_0_.1, s32[1,128]{1,0:T(1,128)} %refs_1_.1, s32[1,128]{1,0:T(1,128)} %refs_2_.1, s32[1,128]{1,0:T(1,128)} %refs_3_.1, f32[1,128]{1,0:T(1,128)} %refs_4_.1, f32[1,128]{1,0:T(1,128)} %refs_5_.1, ...), custom_call_target="tpu_custom_call" | custom-call | tf_op jit(solution)/shard_map/window/pallas_call | solution.py:470
  35.1 1.3 %give.1 = (f32[1,16,128]{2,1,0:T(8,128)}, f32[1,128]{1,0:T(1,128)}) custom-call(f32[24,128]{1,0:T(8,128)} %window.1.both), custom_call_target="tpu_custom_call" | custom-call | tf_op jit(solution)/shard_map/give/pallas_call | solution.py:515

commit v4 on v3

--- a/solution.py
+++ b/solution.py
@@ -435,7 +435,7 @@
         cu[pl.ds(t, 1), :] = current[0:1]
         return iterate, flux_now + half_step * (iterate + voltage)
 
-    lax.fori_loop(0, STEPS, advance, (volts0, flux0))
+    lax.fori_loop(0, STEPS, advance, (volts0, flux0), unroll=4)
 
     reach = four_terms(dot(stack_hi_lo(cu[...]), x2[...], NT))
     placed = dot(stack_hi_lo(vo[...]), put, NT)

time: 36.7 us -> 36.4 us (level)
  no operation moved by 1% of the time
where the time goes in v4:
time: 36.4 us; the launch traced here: 36.1 us
  Pallas kernels  35.5 us (98%)
  between operations  0.64 us (2%)
    pallas_call x1, Pallas kernels, on_device(): pl.pallas_call(functools.partial(kernel, subs, rows, ports, slice_len, ar...  34.2 us
    pallas_call x1, Pallas kernels, on_device(): pl.pallas_call(give, out_shape=(jax.ShapeDtypeStruct((1, STEPS, ports), F...  1.31 us

profile of v4, /device:TPU:0, one launch (start us, length us, event | category | flops | bytes accessed | tf_op | source)
XLA Modules:
  0.0 36.1 jit_solution(3813548499973772210)
XLA Ops:
  0.6 34.2 %window.1.both = f32[24,128]{1,0:T(8,128)} custom-call(f32[1,128,12288]{2,1,0:T(8,128)} %inv.1, f32[1,16,1536]{2,1,0:T(8,128)} %src.1, f32[1,32,128]{2,1,0:T(8,128)} %refs_0_.1, s32[1,128]{1,0:T(1,128)} %refs_1_.1, s32[1,128]{1,0:T(1,128)} %refs_2_.1, s32[1,128]{1,0:T(1,128)} %refs_3_.1, f32[1,128]{1,0:T(1,128)} %refs_4_.1, f32[1,128]{1,0:T(1,128)} %refs_5_.1, ...), custom_call_target="tpu_custom_call" | custom-call | tf_op jit(solution)/shard_map/window/pallas_call | solution.py:470
  34.8 1.3 %give.1 = (f32[1,16,128]{2,1,0:T(8,128)}, f32[1,128]{1,0:T(1,128)}) custom-call(f32[24,128]{1,0:T(8,128)} %window.1.both), custom_call_target="tpu_custom_call" | custom-call | tf_op jit(solution)/shard_map/give/pallas_call | solution.py:515
